TPU v7x, 32 devices: a whole 2x2x4 slice. The times are simulated.
32 devices in a mesh: dp: 8 (over z, x), tensor: 4 (over y, core).
Axes of the slice: x: 2, y: 2, z: 4, core: 2. Of those that a mesh axis runs over, the one named last changes fastest.
Arguments:
- tokens: bfloat16 [16384, 1024], P('dp'), may hold values from -6 to 6
- segments: int32 [16, 1024], P('dp'), may hold values from 0 to 7, never falling along the last dimension, each value on 1 to 512 neighbouring positions
- w_qkv: bfloat16 [1024, 3, 1024], P(None, None, 'tensor'), may hold values from -0.1875 to 0.1875
- head_bias: float32 [2, 1024], P(None, 'tensor'), may hold values from -3 to 3
- w_out: bfloat16 [1024, 1024], P('tensor'), may hold values from -0.75 to 0.75
- w_in: bfloat16 [1024, 4096], P(None, 'tensor'), may hold values from -0.1875 to 0.1875
- unit_bias: float32 [4096], P('tensor'), may hold values from -3 to 3
- w_down: bfloat16 [4096, 1024], P('tensor'), may hold values from -0.09375 to 0.09375
- vectors: float32 [6, 1024], replicated, may hold values from 0.5 to 1.5
- cotangent: bfloat16 [16384, 1024], P('dp'), may hold values from -6 to 6
- err_qkv: float32 [8, 1024, 3, 1024], P('dp', None, None, 'tensor'), may hold values from -80 to 80
- err_out: float32 [8, 1024, 1024], P('dp', 'tensor'), may hold values from -80 to 80
- err_in: float32 [8, 1024, 4096], P('dp', None, 'tensor'), may hold values from -80 to 80
- err_down: float32 [8, 4096, 1024], P('dp', 'tensor'), may hold values from -80 to 80
- basis_qkv: float32 [8, 3, 1024], P(None, None, 'tensor'), may hold values from -6 to 6
- basis_out: float32 [32, 1024], P('tensor'), may hold values from -6 to 6
- basis_in: float32 [8, 4096], P(None, 'tensor'), may hold values from -6 to 6
- basis_down: float32 [32, 1024], P('tensor'), may hold values from -6 to 6
- mom_qkv: float32 [1024, 3, 1024], P(None, None, 'tensor'), may hold values from -5 to 5
- mom_head_bias: float32 [2, 1024], P(None, 'tensor'), may hold values from -10 to 10
- mom_out: float32 [1024, 1024], P('tensor'), may hold values from -5 to 5
- mom_in: float32 [1024, 4096], P(None, 'tensor'), may hold values from -5 to 5
- mom_unit_bias: float32 [4096], P('tensor'), may hold values from -10 to 10
- mom_down: float32 [4096, 1024], P('tensor'), may hold values from -5 to 5
- mom_vectors: float32 [6, 1024], replicated, may hold values from -28 to 28
Outputs:
- layer_out: bfloat16 [16384, 1024], P(('dp', 'tensor'))
- grad_tokens: float32 [16384, 1024], P(('dp', 'tensor'))
- grad_w_qkv: float32 [1024, 3, 1024], P(None, None, 'tensor')
- grad_head_bias: float32 [2, 1024], P(None, 'tensor')
- grad_w_out: float32 [1024, 1024], P('tensor')
- grad_w_in: float32 [1024, 4096], P(None, 'tensor')
- grad_unit_bias: float32 [4096], P('tensor')
- grad_w_down: float32 [4096, 1024], P('tensor')
- grad_vectors: float32 [6, 1024], replicated
- new_err_qkv: float32 [8, 1024, 3, 1024], P('dp', None, None, 'tensor')
- new_err_out: float32 [8, 1024, 1024], P('dp', 'tensor')
- new_err_in: float32 [8, 1024, 4096], P('dp', None, 'tensor')
- new_err_down: float32 [8, 4096, 1024], P('dp', 'tensor')
- new_basis_qkv: float32 [8, 3, 1024], P(None, None, 'tensor')
- new_basis_out: float32 [32, 1024], P('tensor')
- new_basis_in: float32 [8, 4096], P(None, 'tensor')
- new_basis_down: float32 [32, 1024], P('tensor')
- new_mom_qkv: float32 [1024, 3, 1024], P(None, None, 'tensor')
- new_mom_head_bias: float32 [2, 1024], P(None, 'tensor')
- new_mom_out: float32 [1024, 1024], P('tensor')
- new_mom_in: float32 [1024, 4096], P(None, 'tensor')
- new_mom_unit_bias: float32 [4096], P('tensor')
- new_mom_down: float32 [4096, 1024], P('tensor')
- new_mom_vectors: float32 [6, 1024], replicated
- new_w_qkv: float32 [1024, 3, 1024], P(None, None, 'tensor')
- new_head_bias: float32 [2, 1024], P(None, 'tensor')
- new_w_out: float32 [1024, 1024], P('tensor')
- new_w_in: float32 [1024, 4096], P(None, 'tensor')
- new_unit_bias: float32 [4096], P('tensor')
- new_w_down: float32 [4096, 1024], P('tensor')
- new_vectors: float32 [6, 1024], replicated
Inputs may be any that keep to these rules, and one draw needn't show every extreme that they name: `segments`: along a sequence the numbers never fall; each of its 8 documents holds 1 to 512 tokens, and one of them exactly 512.
All inputs are finite; a program needn't handle non-finite values.
Results may differ from a plain program's by a relative error of at most 0.02.
Values may be sent and summed in bfloat16 or wider, within the bound.
A program may use at most 256 MiB of HBM per device.

v0:
```python
from functools import partial
import math
import jax
import jax.numpy as jnp
from jax import lax
from jax.sharding import PartitionSpec as P

DH = 64
PRECISE = lax.Precision.HIGHEST
EPS_NORM = 1e-05
EPS_BASIS = 1e-08
MASKED = -1000000000.0


def norm_forward(values, gain, shift):
    row_mean = jnp.mean(values, axis=-1, keepdims=True)
    centred = values - row_mean
    variance = jnp.mean(centred * centred, axis=-1, keepdims=True)
    inverse = lax.rsqrt(variance + EPS_NORM)
    normed = centred * inverse
    return (normed * gain + shift, normed, inverse)


def norm_backward(grad_norm, normed, inverse, gain):
    scaled_grad = grad_norm * gain
    grad_mean = jnp.mean(scaled_grad, axis=-1, keepdims=True)
    along_norm = jnp.mean(scaled_grad * normed, axis=-1, keepdims=True)
    return inverse * (scaled_grad - grad_mean - normed * along_norm)


def times_trans(left_side, right_side):
    return lax.dot_general(
        left_side, right_side, (((1,), (1,)), ((), ())), preferred_element_type=jnp.float32
    )


def trans_times(left_side, right_side):
    return lax.dot_general(
        left_side, right_side, (((0,), (0,)), ((), ())), preferred_element_type=jnp.float32
    )


def left_of(matrix, factor):
    return lax.dot_general(
        matrix,
        factor,
        (((1,), (1,)), ((), ())),
        precision=PRECISE,
        preferred_element_type=jnp.float32,
    )


def right_of(basis, matrix):
    return lax.dot_general(
        basis,
        matrix,
        (((0,), (0,)), ((), ())),
        precision=PRECISE,
        preferred_element_type=jnp.float32,
    )


def orthonormal(factor):
    columns = []
    for position in range(factor.shape[-1]):
        column = factor[..., position]
        for earlier in columns:
            column = column - jnp.sum(earlier * column, axis=-1, keepdims=True) * earlier
        column = column / (jnp.sqrt(jnp.sum(column * column, axis=-1, keepdims=True)) + EPS_BASIS)
        columns.append(column)
    return jnp.stack(columns, axis=-1)


def masked_scores(queries, key_heads, seg_ids):
    scores = jnp.einsum("qhd,khd->hqk", queries, key_heads, preferred_element_type=jnp.float32)
    same_doc = seg_ids[:, None] == seg_ids[None, :]
    return jnp.where(same_doc[None], scores, MASKED)


def attend_forward(inputs_of):
    queries, key_heads, value_heads, seg_ids = inputs_of
    scores = masked_scores(queries, key_heads, seg_ids)
    highest = jnp.max(scores, axis=-1, keepdims=True)
    powers = jnp.exp(scores - highest)
    denominator = jnp.sum(powers, axis=-1, keepdims=True)
    weights = (powers / denominator).astype(jnp.bfloat16)
    mixed_heads = jnp.einsum(
        "hqk,khd->qhd", weights, value_heads, preferred_element_type=jnp.float32
    )
    return (mixed_heads.astype(jnp.bfloat16), highest[..., 0] + jnp.log(denominator[..., 0]))


def attend_backward(inputs_of):
    queries, key_heads, value_heads, seg_ids, grad_mixed, log_total = inputs_of
    scores = masked_scores(queries, key_heads, seg_ids)
    probability = jnp.exp(scores - log_total[..., None])
    grad_probs = jnp.einsum(
        "qhd,khd->hqk", grad_mixed, value_heads, preferred_element_type=jnp.float32
    )
    centre = jnp.sum(probability * grad_probs, axis=-1, keepdims=True)
    grad_scores = (probability * (grad_probs - centre)).astype(jnp.bfloat16)
    grad_query = jnp.einsum(
        "hqk,khd->qhd", grad_scores, key_heads, preferred_element_type=jnp.float32
    )
    grad_key = jnp.einsum("hqk,qhd->khd", grad_scores, queries, preferred_element_type=jnp.float32)
    grad_value = jnp.einsum(
        "hqk,qhd->khd",
        probability.astype(jnp.bfloat16),
        grad_mixed,
        preferred_element_type=jnp.float32,
    )
    return (
        grad_query.astype(jnp.bfloat16),
        grad_key.astype(jnp.bfloat16),
        grad_value.astype(jnp.bfloat16),
    )


def local(
    tokens,
    segments,
    w_qkv,
    head_bias,
    w_out,
    w_in,
    unit_bias,
    w_down,
    vectors,
    cotangent,
    err_qkv,
    err_out,
    err_in,
    err_down,
    basis_qkv,
    basis_out,
    basis_in,
    basis_down,
    mom_qkv,
    mom_head_bias,
    mom_out,
    mom_in,
    mom_unit_bias,
    mom_down,
    mom_vectors,
):
    token_count, model_width = tokens.shape
    seq_count, length = segments.shape
    head_slab = w_qkv.shape[2]
    head_count = head_slab // DH
    unit_slab = w_in.shape[1]
    rank_size = basis_in.shape[0]
    tensor_size = lax.axis_size("tensor")
    replicas = lax.axis_size("dp")
    share_rows = token_count // tensor_size
    tensor_place = lax.axis_index("tensor")
    row_start = tensor_place * share_rows
    head_scale = 1.0 / math.sqrt(DH)

    def own_rows(values):
        return lax.dynamic_slice_in_dim(values, row_start, share_rows, 0)

    flat_qkv = w_qkv.reshape(model_width, 3 * head_slab)
    projected = jnp.dot(tokens, flat_qkv, preferred_element_type=jnp.float32).reshape(
        token_count, 3, head_slab
    )
    head_shape = (seq_count, length, head_count, DH)
    queries = (
        ((projected[:, 0] + head_bias[0]) * head_scale).astype(jnp.bfloat16).reshape(head_shape)
    )
    key_heads = projected[:, 1].astype(jnp.bfloat16).reshape(head_shape)
    value_heads = (projected[:, 2] + head_bias[1]).astype(jnp.bfloat16).reshape(head_shape)
    mixed_heads, log_total = lax.map(attend_forward, (queries, key_heads, value_heads, segments))
    mixed_flat = mixed_heads.reshape(token_count, head_slab)
    attn_out = (
        lax.psum(jnp.dot(mixed_flat, w_out, preferred_element_type=jnp.float32), "tensor")
        + vectors[0]
    )
    first_norm, first_normed, first_inverse = norm_forward(
        tokens.astype(jnp.float32) + attn_out, vectors[2], vectors[3]
    )
    first_low = first_norm.astype(jnp.bfloat16)
    hidden = jnp.dot(first_low, w_in, preferred_element_type=jnp.float32) + unit_bias
    active, gelu_back = jax.vjp(partial(jax.nn.gelu, approximate=False), hidden)
    active_low = active.astype(jnp.bfloat16)
    grad_out_share = own_rows(cotangent).astype(jnp.float32)
    summed_input = (
        first_norm
        + lax.psum(jnp.dot(active_low, w_down, preferred_element_type=jnp.float32), "tensor")
        + vectors[1]
    )
    second_norm, second_normed, second_inverse = norm_forward(summed_input, vectors[4], vectors[5])
    layer_out = own_rows(second_norm).astype(jnp.bfloat16)
    grad_sum = norm_backward(
        cotangent.astype(jnp.float32), second_normed, second_inverse, vectors[4]
    )
    grad_branch = grad_sum.astype(jnp.bfloat16)
    second_share = own_rows(second_normed)
    grad_w_down = trans_times(active_low, grad_branch)
    grad_active = times_trans(grad_branch, w_down)
    grad_hidden = gelu_back(grad_active)[0].astype(jnp.bfloat16)
    grad_w_in = trans_times(first_low, grad_hidden)
    grad_units = jnp.sum(grad_hidden.astype(jnp.float32), axis=0)
    grad_first = lax.psum(times_trans(grad_hidden, w_in), "tensor") + grad_sum
    grad_h1 = norm_backward(grad_first, first_normed, first_inverse, vectors[2])
    grad_attn = grad_h1.astype(jnp.bfloat16)
    grad_first_share = own_rows(grad_first)
    first_normed_share = own_rows(first_normed)
    grad_h1_share = own_rows(grad_h1)
    grad_w_out = trans_times(mixed_flat, grad_attn)
    grad_mixed = times_trans(grad_attn, w_out).astype(jnp.bfloat16).reshape(head_shape)
    grad_query, grad_key, grad_value = lax.map(
        attend_backward, (queries, key_heads, value_heads, segments, grad_mixed, log_total)
    )
    grad_query = (
        grad_query.reshape(token_count, head_slab).astype(jnp.float32) * head_scale
    ).astype(jnp.bfloat16)
    grad_key = grad_key.reshape(token_count, head_slab)
    grad_value = grad_value.reshape(token_count, head_slab)
    grad_projected = jnp.stack([grad_query, grad_key, grad_value], axis=1).reshape(
        token_count, 3 * head_slab
    )
    grad_w_qkv = trans_times(tokens, grad_projected)
    grad_heads = jnp.stack(
        [
            jnp.sum(grad_query.astype(jnp.float32), axis=0),
            jnp.sum(grad_value.astype(jnp.float32), axis=0),
        ]
    )
    grad_tokens = (
        lax.psum_scatter(
            times_trans(grad_projected, flat_qkv).astype(jnp.bfloat16),
            "tensor",
            scatter_dimension=0,
            tiled=True,
        ).astype(jnp.float32)
        + grad_h1_share
    )
    local_vectors = jnp.stack(
        [
            jnp.sum(own_rows(grad_attn).astype(jnp.float32), axis=0),
            jnp.sum(own_rows(grad_branch).astype(jnp.float32), axis=0),
            jnp.sum(grad_first_share * first_normed_share, axis=0),
            jnp.sum(grad_first_share, axis=0),
            jnp.sum(grad_out_share * second_share, axis=0),
            jnp.sum(grad_out_share, axis=0),
        ]
    )
    zero_index = jnp.zeros((), jnp.int32)
    head_full = lax.dynamic_update_slice(
        jnp.zeros((2, head_slab * tensor_size), jnp.float32),
        grad_heads,
        (zero_index, tensor_place * head_slab),
    )
    unit_full = lax.dynamic_update_slice(
        jnp.zeros((unit_slab * tensor_size,), jnp.float32), grad_units, (tensor_place * unit_slab,)
    )
    vector_sum, head_sum, unit_sum = lax.psum(
        (local_vectors, head_full, unit_full), ("dp", "tensor")
    )
    grad_vectors = vector_sum / replicas
    grad_head_bias = (
        lax.dynamic_slice_in_dim(head_sum, tensor_place * head_slab, head_slab, 1) / replicas
    )
    grad_unit_bias = (
        lax.dynamic_slice_in_dim(unit_sum, tensor_place * unit_slab, unit_slab, 0) / replicas
    )
    combined_qkv = grad_w_qkv + err_qkv[0].reshape(model_width, 3 * head_slab)
    combined_out = grad_w_out + err_out[0]
    combined_in = grad_w_in + err_in[0]
    combined_down = grad_w_down + err_down[0]
    left_qkv, left_out, left_in, left_down = (
        lax.psum(
            left_of(combined_qkv, basis_qkv.reshape(rank_size, 3 * head_slab)).astype(jnp.bfloat16),
            "dp",
        ).astype(jnp.float32),
        lax.psum(left_of(combined_out, basis_out).astype(jnp.bfloat16), "dp").astype(jnp.float32),
        lax.psum(left_of(combined_in, basis_in).astype(jnp.bfloat16), "dp").astype(jnp.float32),
        lax.psum(left_of(combined_down, basis_down).astype(jnp.bfloat16), "dp").astype(jnp.float32),
    )
    ortho_qkv = orthonormal(left_qkv / replicas)
    ortho_out = orthonormal(left_out / replicas)
    ortho_in = orthonormal(left_in / replicas)
    ortho_down = orthonormal(left_down / replicas)
    right_qkv, right_out, right_in, right_down = (
        lax.psum(right_of(ortho_qkv, combined_qkv).astype(jnp.bfloat16), "dp").astype(jnp.float32),
        lax.psum(right_of(ortho_out, combined_out).astype(jnp.bfloat16), "dp").astype(jnp.float32),
        lax.psum(right_of(ortho_in, combined_in).astype(jnp.bfloat16), "dp").astype(jnp.float32),
        lax.psum(right_of(ortho_down, combined_down).astype(jnp.bfloat16), "dp").astype(
            jnp.float32
        ),
    )
    right_qkv = right_qkv / replicas
    right_out = right_out / replicas
    right_in = right_in / replicas
    right_down = right_down / replicas
    rank_qkv = jnp.dot(ortho_qkv, right_qkv, precision=PRECISE)
    rank_out = jnp.dot(ortho_out, right_out, precision=PRECISE)
    rank_in = jnp.dot(ortho_in, right_in, precision=PRECISE)
    rank_down = jnp.dot(ortho_down, right_down, precision=PRECISE)
    reduced_qkv = rank_qkv.reshape(model_width, 3, head_slab)
    new_err_qkv = (combined_qkv - rank_qkv).reshape(1, model_width, 3, head_slab)
    new_err_out = (combined_out - rank_out)[None]
    new_err_in = (combined_in - rank_in)[None]
    new_err_down = (combined_down - rank_down)[None]
    new_basis_qkv = right_qkv.reshape(rank_size, 3, head_slab)
    step_rate = 0.3 * math.sqrt(replicas / token_count)
    new_mom_qkv = 0.9 * mom_qkv + reduced_qkv
    new_mom_head_bias = 0.9 * mom_head_bias + grad_head_bias
    new_mom_out = 0.9 * mom_out + rank_out
    new_mom_in = 0.9 * mom_in + rank_in
    new_mom_unit_bias = 0.9 * mom_unit_bias + grad_unit_bias
    new_mom_down = 0.9 * mom_down + rank_down
    new_mom_vectors = 0.9 * mom_vectors + grad_vectors
    new_w_qkv = w_qkv.astype(jnp.float32) - step_rate * new_mom_qkv
    new_head_bias = head_bias - step_rate * new_mom_head_bias
    new_w_out = w_out.astype(jnp.float32) - step_rate * new_mom_out
    new_w_in = w_in.astype(jnp.float32) - step_rate * new_mom_in
    new_unit_bias = unit_bias - step_rate * new_mom_unit_bias
    new_w_down = w_down.astype(jnp.float32) - step_rate * new_mom_down
    new_vectors = vectors - step_rate * new_mom_vectors
    return (
        layer_out,
        grad_tokens,
        reduced_qkv,
        grad_head_bias,
        rank_out,
        rank_in,
        grad_unit_bias,
        rank_down,
        grad_vectors,
        new_err_qkv,
        new_err_out,
        new_err_in,
        new_err_down,
        new_basis_qkv,
        right_out,
        right_in,
        right_down,
        new_mom_qkv,
        new_mom_head_bias,
        new_mom_out,
        new_mom_in,
        new_mom_unit_bias,
        new_mom_down,
        new_mom_vectors,
        new_w_qkv,
        new_head_bias,
        new_w_out,
        new_w_in,
        new_unit_bias,
        new_w_down,
        new_vectors,
    )


def solution(mesh):
    in_specs = (
        P("dp", None),
        P("dp", None),
        P(None, None, "tensor"),
        P(None, "tensor"),
        P("tensor", None),
        P(None, "tensor"),
        P("tensor"),
        P("tensor", None),
        P(),
        P("dp", None),
        P("dp", None, None, "tensor"),
        P("dp", "tensor", None),
        P("dp", None, "tensor"),
        P("dp", "tensor", None),
        P(None, None, "tensor"),
        P("tensor", None),
        P(None, "tensor"),
        P("tensor", None),
        P(None, None, "tensor"),
        P(None, "tensor"),
        P("tensor", None),
        P(None, "tensor"),
        P("tensor"),
        P("tensor", None),
        P(),
    )
    out_specs = (
        P(("dp", "tensor"), None),
        P(("dp", "tensor"), None),
        P(None, None, "tensor"),
        P(None, "tensor"),
        P("tensor", None),
        P(None, "tensor"),
        P("tensor"),
        P("tensor", None),
        P(),
        P("dp", None, None, "tensor"),
        P("dp", "tensor", None),
        P("dp", None, "tensor"),
        P("dp", "tensor", None),
        P(None, None, "tensor"),
        P("tensor", None),
        P(None, "tensor"),
        P("tensor", None),
        P(None, None, "tensor"),
        P(None, "tensor"),
        P("tensor", None),
        P(None, "tensor"),
        P("tensor"),
        P("tensor", None),
        P(),
        P(None, None, "tensor"),
        P(None, "tensor"),
        P("tensor", None),
        P(None, "tensor"),
        P("tensor"),
        P("tensor", None),
        P(),
    )
    return jax.shard_map(local, mesh=mesh, in_specs=in_specs, out_specs=out_specs, check_vma=False)
```

profile of v0, /device:TPU:12, one launch (start us, length us, event | category | flops | bytes accessed | tf_op | source)
XLA Modules:
  0.0 1268.8 jit_solution(10177957480828531079)
XLA Ops:
  44.9 51.5 %while.26 = (s32[]{:T(128)}, bf16[2,1024,4,64]{1,3,2,0:T(8,128)(2,1)}, f32[2,4,1024]{2,1,0:T(4,128)S(1)}, bf16[2,1024,4,64]{1,3,2,0:T(8,128)(2,1)}, s32[2,1024]{...) while((s32[]{:T(128)}, ...), condition=%wide.region_3.4_spmd, body=%wide.region_0.3_spmd.sunk | while | flops 1112797184 | bytes 56768612 | solution.py:172
  53.1 8.8 fusion.154
  61.8 8.9 fusion.155
  78.7 8.8 fusion.154
  87.5 8.9 fusion.155
  106.4 153.3 %all-reduce.7.cloned.1.call-done = f32[2048,1024]{1,0:T(8,128)} async-done(((f32[2048,1024]{1,0:T(8,128)}), f32[2048,1024]{1,0:T(8,128)}) %all-reduce.7.cloned.1.call-update) | async-done | bytes 8388624 | tf_op jit(solution)/shard_map/psum | solution.py:175
  271.8 24.4 %multiply_convert_fusion.1 = (bf16[2048,1024]{1,0:T(8,128)(2,1)S(1)}, f32[2048,1024]{1,0:T(8,128)}, f32[2048,1024]{1,0:T(8,128)}) fusion(f32[1024]{0:T(1024)S(1)} %copy-done.65, bf16[1024,1024]{1,0:T(8,128)(2,1)S(1)} %copy-done.37, f32[2048,1024]{1,0:T(8,128)S(1)} %subtract_multiply_fusion.3, f32[1024]{0:T(1024)S(1)} %bitcast.353, f32[1024]{0:T(1024)S(1)} %bitcast.281), kind=kOutput, calls=%fused_computation.74 | convolution fusion | flops 4439670784 | bytes 31469568 | tf_op jit(solution)/shard_map/dot_general | solution.py:182
  304.9 153.1 %all-reduce.9.cloned.1.call-done = f32[2048,1024]{1,0:T(8,128)} async-done(((f32[2048,1024]{1,0:T(8,128)}), f32[2048,1024]{1,0:T(8,128)}) %all-reduce.9.cloned.1.call-update) | async-done | bytes 8388624 | tf_op jit(solution)/shard_map/psum | solution.py:188
  473.5 13.2 %convert_reduce_fusion = (f32[1024]{0:T(1024)S(1)}, bf16[2048,1024]{1,0:T(8,128)(2,1)S(1)}) fusion(f32[2048,1024]{1,0:T(8,128)} %get-tuple-element.569, f32[2048,1024]{1,0:T(8,128)} %get-tuple-element.620, f32[1024]{0:T(1024)S(1)} %copy-done.65, bf16[2048,1024]{1,0:T(8,128)(2,1)S(1)} %fusion.74, bf16[1024,1024]{1,0:T(8,128)(2,1)S(1)} %copy-done.39), kind=kOutput, calls=%fused_computation.64 | convolution fusion | flops 4330617856 | bytes 27271168 | tf_op jit(solution)/shard_map/dot_general | solution.py:32
  505.4 9.5 bitcast_add_fusion
  532.2 116.6 %all-reduce.11.cloned.1.call-done = f32[2048,1024]{1,0:T(8,128)} async-done(((f32[2048,1024]{1,0:T(8,128)}), f32[2048,1024]{1,0:T(8,128)}) %all-reduce.11.cloned.1.call-update) | async-done | bytes 8388624 | tf_op jit(solution)/shard_map/psum | solution.py:203
  648.8 11.4 multiply_reduce_fusion.5
  660.3 9.5 fusion.76
  683.1 95.2 %while.27 = (s32[]{:T(128)}, bf16[2,1024,4,64]{1,3,2,0:T(8,128)(2,1)}, bf16[2,1024,4,64]{1,3,2,0:T(8,128)(2,1)}, bf16[2,1024,4,64]{1,3,2,0:T(8,128)(2,1)}, bf16[...) while((s32[]{:T(128)}, ...), condition=%wide.region_17.18_spmd, body=%wide.region_15.17_spmd.sunk | while | flops 2736517120 | bytes 219284944 | solution.py:211
  684.2 9.5 fusion.164
  693.7 8.9 fusion.167
  702.6 14.7 %multiply_reduce_fusion.152 = (f32[4,1024]{1,0:T(4,128)S(1)}, f32[4,1024,1024]{1,2,0:T(8,128)}) fusion(f32[4,1024,1024]{1,2,0:T(8,128)} %fusion.164, f32[4,1024]{1,0:T(4,128)S(1)} %dynamic-slice_bitcast_fusion.2, pred[1024,1024]{0,1:T(8,128)(4,1)} %copy-done.2, bf16[2,1024,4,64]{1,3,2,0:T(8,128)(2,1)} %get-tuple-element.793, s32[]{:T(128)S(6)} %copy.165, ...), kind=kOutput, calls=%fused_computation.22.clone.1 | convolution fusion | flops 553644032 | bytes 35685376 | tf_op jit(solution)/shard_map/while/body/eval_jaxpr/qhd,khd->hqk/dot_general | solution.py:97
  717.4 8.2 multiply_convert_fusion.5
  731.6 9.5 fusion.164
  741.2 8.9 fusion.167
  750.0 14.7 %multiply_reduce_fusion.152 = (f32[4,1024]{1,0:T(4,128)S(1)}, f32[4,1024,1024]{1,2,0:T(8,128)}) fusion(f32[4,1024,1024]{1,2,0:T(8,128)} %fusion.164, f32[4,1024]{1,0:T(4,128)S(1)} %dynamic-slice_bitcast_fusion.2, pred[1024,1024]{0,1:T(8,128)(4,1)} %copy-done.2, bf16[2,1024,4,64]{1,3,2,0:T(8,128)(2,1)} %get-tuple-element.793, s32[]{:T(128)S(6)} %copy.165, ...), kind=kOutput, calls=%fused_computation.22.clone.1 | convolution fusion | flops 553644032 | bytes 35685376 | tf_op jit(solution)/shard_map/while/body/eval_jaxpr/qhd,khd->hqk/dot_general | solution.py:97
  764.8 8.2 multiply_convert_fusion.5
  818.0 7.5 bitcast_add_fusion.2
  827.3 35.2 %all-reduce.2 = (bf16[1024,8]{0,1:T(8,128)(2,1)S(1)}, bf16[256,8]{0,1:T(8,128)(2,1)S(1)}, bf16[1024,8]{0,1:T(8,128)(2,1)S(1)}, bf16[1024,8]{0,1:T(8,128)(2,1)S(1)}) all-reduce(bf16[1024,8]{0,1:T(8,128)(2,1)S(1)} %convolution_convert_fusion.8, ...), channel_id=1, replica_groups=mesh['dp'=8,'tensor'=4] {'dp'}, use_global_device_ids=true, to_apply=%region_19.20 | all-reduce | flops 26624 | bytes 106496 | tf_op jit(solution)/shard_map/psum | solution.py:272
  1040.1 17.5 %subtract_divide_fusion.21 = (f32[256,1]{0,1:T(1,128)S(1)}, f32[256,1]{0,1:T(1,128)S(1)}, f32[256,1]{0,1:T(1,128)S(1)}, f32[256,1]{0,1:T(1,128)S(1)}, f32[256,1]...) fusion(f32[256,1]{0,1:T(1,128)S(1)} %get-tuple-element.613, f32[]{:T(128)S(6)} %add.371, ...), kind=kLoop, calls=%fused_computation.402 | loop fusion | flops 16128 | bytes 15500 | tf_op jit(solution)/shard_map/div | solution.py:69
  1057.7 18.2 %subtract_divide_fusion.14 = (f32[1024,1]{0,1:T(1,128)S(1)}, f32[1024,1]{0,1:T(1,128)S(1)}, f32[1024,1]{0,1:T(1,128)S(1)}, f32[1024,1]{0,1:T(1,128)S(1)}, f32[10...) fusion(f32[1024,1]{0,1:T(1,128)S(1)} %get-tuple-element.599, f32[]{:T(128)S(6)} %add.361, ...), kind=kLoop, calls=%fused_computation.300 | loop fusion | flops 64512 | bytes 61580 | tf_op jit(solution)/shard_map/div | solution.py:69
  1075.9 17.4 %subtract_divide_fusion.7 = (f32[1024,1]{0,1:T(1,128)S(1)}, f32[1024,1]{0,1:T(1,128)S(1)}, f32[1024,1]{0,1:T(1,128)S(1)}, f32[1024,1]{0,1:T(1,128)S(1)}, f32[102...) fusion(f32[1024,1]{0,1:T(1,128)S(1)} %get-tuple-element.591, f32[]{:T(128)S(6)} %add.380, ...), kind=kLoop, calls=%fused_computation.230 | loop fusion | flops 64512 | bytes 61580 | tf_op jit(solution)/shard_map/div | solution.py:69
  1093.3 17.5 %subtract_divide_fusion = (f32[1024,1]{0,1:T(1,128)S(1)}, f32[1024,1]{0,1:T(1,128)S(1)}, f32[1024,1]{0,1:T(1,128)S(1)}, f32[1024,1]{0,1:T(1,128)S(1)}, f32[1024,...) fusion(f32[1024,1]{0,1:T(1,128)S(1)} %get-tuple-element.583, f32[]{:T(128)S(6)} %add.390, ...), kind=kLoop, calls=%fused_computation.159 | loop fusion | flops 64512 | bytes 61580 | tf_op jit(solution)/shard_map/div | solution.py:69
  1121.9 33.7 %all-reduce.1 = (bf16[8,768]{1,0:T(8,128)(2,1)S(1)}, bf16[8,1024]{1,0:T(8,128)(2,1)S(1)}, bf16[8,1024]{1,0:T(8,128)(2,1)S(1)}, bf16[8,1024]{1,0:T(8,128)(2,1)S(1)}) all-reduce(bf16[8,768]{1,0:T(8,128)(2,1)S(1)} %convolution_convert_fusion.9, ...), channel_id=1, replica_groups=mesh['dp'=8,'tensor'=4] {'dp'}, use_global_device_ids=true, to_apply=%region_56.57 | all-reduce | flops 30720 | bytes 122880 | tf_op jit(solution)/shard_map/psum | solution.py:285
  1172.0 43.4 %all-reduce = (f32[2,1024]{1,0:T(2,128)S(1)}, f32[4096]{0:T(1024)S(1)}, f32[6,1024]{1,0:T(8,128)S(1)}) all-reduce(f32[2,1024]{1,0:T(2,128)S(1)} %constant_dynamic-update-slice_fusion.3, f32[4096]{0:T(1024)S(1)} %copy-done.56, f32[6,1024]{1,0:T(8,128)S(1)} %stack.44), channel_id=1, replica_groups=mesh['dp'=8,'tensor'=4] {'dp','tensor'}, use_global_device_ids=true, to_apply=%region_59.60 | all-reduce | flops 12288 | bytes 98304 | tf_op jit(solution)/shard_map/psum | solution.py:257
  1234.5 12.2 multiply_subtract_fusion.1
  1246.7 11.5 multiply_subtract_fusion
  (376 shorter events, 408.0 us)
Async XLA Ops:
  7.2 509.6 %copy-start = (f32[8,1024]{1,0:T(8,128)S(1)}, f32[8,1024]{1,0:T(8,128)}, u32[]{:S(2)}) copy-start(f32[8,1024]{1,0:T(8,128)} %param.46) | copy-start | bytes 98308
  7.2 252.4 %all-reduce.7.cloned.1.call-start = ((), (), s32[]{:S(2)}) async-start(), calls=%async_computation.1 | async-start | bytes 16777216 | tf_op jit(solution)/shard_map/psum | solution.py:175
  106.3 351.7 %all-reduce.9.cloned.1.call-start = ((), (), s32[]{:S(2)}) async-start(), calls=%async_computation.2 | async-start | bytes 16777216 | tf_op jit(solution)/shard_map/psum | solution.py:188
  271.7 24.5 %copy-start.3 = (f32[2048,1024]{1,0:T(8,128)}, f32[2048,1024]{1,0:T(8,128)S(1)}, u32[]{:S(2)}) copy-start(f32[2048,1024]{1,0:T(8,128)S(1)} %subtract_multiply_fusion.3) | copy-start | bytes 25165828
  271.8 26.4 %copy-start.38 = (bf16[1024,1024]{1,0:T(8,128)(2,1)S(1)}, bf16[1024,1024]{1,0:T(8,128)(2,1)}, u32[]{:S(2)}) copy-start(bf16[1024,1024]{1,0:T(8,128)(2,1)} %param.36) | copy-start | bytes 6291460
  304.9 343.9 %all-reduce.11.cloned.1.call-start = ((), (), s32[]{:S(2)}) async-start(), calls=%async_computation.3 | async-start | bytes 16777216 | tf_op jit(solution)/shard_map/psum | solution.py:203
  495.6 762.6 %reduce-scatter.2.cloned.1.call-start = ((), (), s32[]{:S(2)}) async-start(), calls=%async_computation.4 | async-start | bytes 5242880 | tf_op jit(solution)/shard_map/reduce_scatter | solution.py:230
  500.8 20.3 %slice-start.4 = ((s8[8388608]{0:T(1024)(128)(4,1)}), s8[4194304]{0:T(1024)(128)(4,1)S(1)}, s32[]{:S(2)}) async-start(s8[8388608]{0:T(1024)(128)(4,1)} %bitcast.240), calls=%async_computation.9 | async-start | bytes 8388608
  505.4 15.6 %slice-start.5 = ((s8[8388608]{0:T(1024)(128)(4,1)}), s8[4194304]{0:T(1024)(128)(4,1)S(1)}, s32[]{:S(2)}) async-start(s8[8388608]{0:T(1024)(128)(4,1)} %bitcast.240), calls=%async_computation.10 | async-start | bytes 8388608
  505.4 15.6 %copy-start.69 = (f32[1,1024,1024]{2,1,0:T(8,128)S(1)}, f32[1,1024,1024]{2,1,0:T(8,128)}, u32[]{:S(2)}) copy-start(f32[1,1024,1024]{2,1,0:T(8,128)} %param.41) | copy-start | bytes 12582916
  505.4 15.6 %copy-start.71 = (bf16[2048,1024]{1,0:T(8,128)(2,1)S(1)}, bf16[2048,1024]{1,0:T(8,128)(2,1)}, u32[]{:S(2)}) copy-start(bf16[2048,1024]{1,0:T(8,128)(2,1)} %copy-done.70) | copy-start | bytes 12582916
  532.2 128.1 %copy-start.52 = (f32[2048]{0:T(1024)S(1)}, f32[2048]{0:T(1024)}, u32[]{:S(2)}) copy-start(f32[2048]{0:T(1024)} %copy-done.51) | copy-start | bytes 24580
  693.7 23.6 %slice-start = ((s8[16777216]{0:T(1024)(128)(4,1)}), s8[4194304]{0:T(1024)(128)(4,1)S(1)}, s32[]{:S(2)}) async-start(s8[16777216]{0:T(1024)(128)(4,1)} %bitcast.238), calls=%async_computation.5 | async-start | bytes 8388608 | tf_op jit(solution)/shard_map/while
  693.7 23.6 %slice-start.1 = ((s8[16777216]{0:T(1024)(128)(4,1)}), s8[4194304]{0:T(1024)(128)(4,1)S(1)}, s32[]{:S(2)}) async-start(s8[16777216]{0:T(1024)(128)(4,1)} %bitcast.238), calls=%async_computation.6 | async-start | bytes 8388608 | tf_op jit(solution)/shard_map/while
  702.6 14.7 %slice-start.2 = ((s8[16777216]{0:T(1024)(128)(4,1)}), s8[4194304]{0:T(1024)(128)(4,1)S(1)}, s32[]{:S(2)}) async-start(s8[16777216]{0:T(1024)(128)(4,1)} %bitcast.238), calls=%async_computation.7 | async-start | bytes 8388608 | tf_op jit(solution)/shard_map/while
  702.6 14.7 %slice-start.3 = ((s8[16777216]{0:T(1024)(128)(4,1)}), s8[4194304]{0:T(1024)(128)(4,1)S(1)}, s32[]{:S(2)}) async-start(s8[16777216]{0:T(1024)(128)(4,1)} %bitcast.238), calls=%async_computation.8 | async-start | bytes 8388608 | tf_op jit(solution)/shard_map/while
  741.2 23.6 %slice-start = ((s8[16777216]{0:T(1024)(128)(4,1)}), s8[4194304]{0:T(1024)(128)(4,1)S(1)}, s32[]{:S(2)}) async-start(s8[16777216]{0:T(1024)(128)(4,1)} %bitcast.238), calls=%async_computation.5 | async-start | bytes 8388608 | tf_op jit(solution)/shard_map/while
  741.2 23.6 %slice-start.1 = ((s8[16777216]{0:T(1024)(128)(4,1)}), s8[4194304]{0:T(1024)(128)(4,1)S(1)}, s32[]{:S(2)}) async-start(s8[16777216]{0:T(1024)(128)(4,1)} %bitcast.238), calls=%async_computation.6 | async-start | bytes 8388608 | tf_op jit(solution)/shard_map/while
  750.0 14.7 %slice-start.2 = ((s8[16777216]{0:T(1024)(128)(4,1)}), s8[4194304]{0:T(1024)(128)(4,1)S(1)}, s32[]{:S(2)}) async-start(s8[16777216]{0:T(1024)(128)(4,1)} %bitcast.238), calls=%async_computation.7 | async-start | bytes 8388608 | tf_op jit(solution)/shard_map/while
  750.0 14.7 %slice-start.3 = ((s8[16777216]{0:T(1024)(128)(4,1)}), s8[4194304]{0:T(1024)(128)(4,1)S(1)}, s32[]{:S(2)}) async-start(s8[16777216]{0:T(1024)(128)(4,1)} %bitcast.238), calls=%async_computation.8 | async-start | bytes 8388608 | tf_op jit(solution)/shard_map/while
  1160.2 55.3 %copy-start.64 = (f32[2,256]{1,0:T(2,128)S(1)}, f32[2,256]{1,0:T(2,128)}, u32[]{:S(2)}) copy-start(f32[2,256]{1,0:T(2,128)} %param.32) | copy-start | bytes 6148
  1160.2 55.3 %copy-start.68 = (f32[2,256]{1,0:T(2,128)S(1)}, f32[2,256]{1,0:T(2,128)}, u32[]{:S(2)}) copy-start(f32[2,256]{1,0:T(2,128)} %param.48) | copy-start | bytes 6148
  1160.2 55.9 %copy-start.66 = (f32[1024]{0:T(1024)S(1)}, f32[1024]{0:T(1024)}, u32[]{:S(2)}) copy-start(f32[1024]{0:T(1024)} %param.35) | copy-start | bytes 12292
  1160.3 55.8 %copy-start.67 = (f32[1024]{0:T(1024)S(1)}, f32[1024]{0:T(1024)}, u32[]{:S(2)}) copy-start(f32[1024]{0:T(1024)} %param.51) | copy-start | bytes 12292
  1160.3 57.1 %copy-start.50 = (f32[6,1024]{1,0:T(8,128)S(1)}, f32[6,1024]{1,0:T(8,128)}, u32[]{:S(2)}) copy-start(f32[6,1024]{1,0:T(8,128)} %param.37) | copy-start | bytes 73732
  1160.3 57.1 %copy-start.59 = (f32[6,1024]{1,0:T(8,128)S(1)}, f32[6,1024]{1,0:T(8,128)}, u32[]{:S(2)}) copy-start(f32[6,1024]{1,0:T(8,128)} %param.53) | copy-start | bytes 73732
  1166.3 64.8 %copy-start.19 = (f32[1024,3,256]{2,0,1:T(8,128)}, f32[1024,3,256]{2,0,1:T(8,128)S(1)}, u32[]{:S(2)}) copy-start(f32[1024,3,256]{2,0,1:T(8,128)S(1)} %copy.125) | copy-start | bytes 9437188
  1217.3 13.8 %copy-start.33 = (f32[1024,3,256]{2,0,1:T(8,128)S(1)}, f32[1024,3,256]{2,0,1:T(8,128)}, u32[]{:S(2)}) copy-start(f32[1024,3,256]{2,0,1:T(8,128)} %param.47) | copy-start | bytes 9437188
  1217.3 17.2 %copy-start.48 = (f32[8,1024]{1,0:T(8,128)}, f32[8,1024]{1,0:T(8,128)S(1)}, u32[]{:S(2)}) copy-start(f32[8,1024]{1,0:T(8,128)S(1)} %convert_multiply_fusion.6) | copy-start | bytes 98308
  1217.4 17.1 %copy-start.46 = (f32[8,1024]{1,0:T(8,128)}, f32[8,1024]{1,0:T(8,128)S(1)}, u32[]{:S(2)}) copy-start(f32[8,1024]{1,0:T(8,128)S(1)} %convert_multiply_fusion.4) | copy-start | bytes 98308
  1217.4 17.1 %copy-start.47 = (f32[8,1024]{1,0:T(8,128)}, f32[8,1024]{1,0:T(8,128)S(1)}, u32[]{:S(2)}) copy-start(f32[8,1024]{1,0:T(8,128)S(1)} %convert_multiply_fusion.2) | copy-start | bytes 98308
  1246.7 15.1 %copy-start.1 = (f32[8,1024]{1,0:T(8,128)S(1)}, f32[8,1024]{1,0:T(8,128)}, u32[]{:S(2)}) copy-start(f32[8,1024]{1,0:T(8,128)} %param.46) | copy-start | bytes 98308
  (62 other events, 430.4 us)
Sparse Core Ops, SparseCore 0:
  106.4 153.2 all-reduce.6
  305.0 153.0 all-reduce.8
  495.7 152.9 all-reduce.10
  1029.7 43.5 reduce-scatter.1
where the time goes:
time: 1280 us; the launch traced here: 1270 us
  waiting for transfers between devices  423 us (33%)
  other arithmetic  359 us (28%)
  matrix products  242 us (19%)
  blocking collectives  112 us (9%)
  local copies, waits for them, and re-layouts  94.7 us (7%)
  between operations  37 us (3%)
    psum x1, waiting for transfers between devices, local(): lax.psum(jnp.dot(mixed_flat, w_out, preferred_element_type=jnp.float32),...  153 us
    psum x1, waiting for transfers between devices, local(): lax.psum(jnp.dot(active_low, w_down, preferred_element_type=jnp.float32),...  153 us
    reduce_sum x40, other arithmetic, orthonormal(): jnp.sum(earlier * column, axis=-1, keepdims=True) * earlier  122 us
    psum x1, waiting for transfers between devices, local(): grad_first = lax.psum(times_trans(grad_hidden, w_in), 'tensor') + grad_sum  117 us
    div x4, other arithmetic, orthonormal(): column / (jnp.sqrt(jnp.sum(column * column, axis=-1, keepdims=True)) + EP...  70.6 us
    psum x1, blocking collectives, local(): lax.psum((local_vectors, head_full, unit_full), ('dp', 'tensor'))  43.4 us
    psum x1, blocking collectives, local(): lax.psum(left_of(combined_qkv, basis_qkv.reshape(rank_size, 3 * head_slab...  35.2 us
    reduce_sum x20, other arithmetic, orthonormal(): jnp.sum(column * column, axis=-1, keepdims=True)  33.8 us
  transfers between devices with their start and end apart: 4, of which 3 were waited for; matrix products, arithmetic and copies ran while one was open for 14% of the time, Pallas kernels for 0%

commit v1 on v0

--- a/solution.py
+++ b/solution.py
@@ -282,7 +282,9 @@
     ortho_in = orthonormal(left_in / replicas)
     ortho_down = orthonormal(left_down / replicas)
     right_qkv, right_out, right_in, right_down = (
-        lax.psum(right_of(ortho_qkv, combined_qkv).astype(jnp.bfloat16), "dp").astype(jnp.float32),
+        jnp.sum(
+            lax.all_gather(right_of(ortho_qkv, combined_qkv).astype(jnp.bfloat16), "dp"), axis=0
+        ).astype(jnp.float32),
         lax.psum(right_of(ortho_out, combined_out).astype(jnp.bfloat16), "dp").astype(jnp.float32),
         lax.psum(right_of(ortho_in, combined_in).astype(jnp.bfloat16), "dp").astype(jnp.float32),
         lax.psum(right_of(ortho_down, combined_down).astype(jnp.bfloat16), "dp").astype(

time: 1280 us -> 1350 us (1.055)
  waiting for transfers between devices: 423 us -> 490 us
    psum x0 -> x1, waiting for transfers between devices: none -> 67.3 us  [local(): lax.psum(left_of(combined_qkv, basis_qkv.reshape(rank_size, 3 * head_slab...]
    psum x2 -> x1, blocking collectives: 68.9 us -> 35.1 us  [local(): lax.psum(left_of(combined_out, basis_out).astype(jnp.bfloat16), 'dp')]
    all_gather x0 -> x1, blocking collectives: none -> 27.7 us  [local(): lax.all_gather(right_of(ortho_qkv, combined_qkv).astype(jnp.bfloat16), 'dp')]
    unnamed x139 -> x147, local copies, waits for them, and re-layouts: 33.3 us -> 31.3 us
  transfers between devices with their start and end apart: 4 -> 5, of which waited for: 3 -> 4; matrix products, arithmetic and copies ran while one was open for 14% -> 11% of each run, Pallas kernels for 0% -> 0%
where the time goes in v1:
time: 1350 us; the launch traced here: 1330 us
  waiting for transfers between devices  490 us (36%)
  other arithmetic  359 us (27%)
  matrix products  245 us (18%)
  blocking collectives  106 us (8%)
  local copies, waits for them, and re-layouts  92.6 us (7%)
  between operations  37 us (3%)
    psum x1, waiting for transfers between devices, local(): lax.psum(jnp.dot(mixed_flat, w_out, preferred_element_type=jnp.float32),...  153 us
    psum x1, waiting for transfers between devices, local(): lax.psum(jnp.dot(active_low, w_down, preferred_element_type=jnp.float32),...  153 us
    reduce_sum x40, other arithmetic, orthonormal(): jnp.sum(earlier * column, axis=-1, keepdims=True) * earlier  123 us
    psum x1, waiting for transfers between devices, local(): grad_first = lax.psum(times_trans(grad_hidden, w_in), 'tensor') + grad_sum  117 us
    div x4, other arithmetic, orthonormal(): column / (jnp.sqrt(jnp.sum(column * column, axis=-1, keepdims=True)) + EP...  71.5 us
    psum x1, waiting for transfers between devices, local(): lax.psum(left_of(combined_qkv, basis_qkv.reshape(rank_size, 3 * head_slab...  67.3 us
    psum x1, blocking collectives, local(): lax.psum((local_vectors, head_full, unit_full), ('dp', 'tensor'))  43.7 us
    psum x1, blocking collectives, local(): lax.psum(left_of(combined_out, basis_out).astype(jnp.bfloat16), 'dp')  35.1 us
  transfers between devices with their start and end apart: 5, of which 4 were waited for; matrix products, arithmetic and copies ran while one was open for 11% of the time, Pallas kernels for 0%

profile of v1, /device:TPU:12, one launch (start us, length us, event | category | flops | bytes accessed | tf_op | source)
XLA Modules:
  0.0 1332.1 jit_solution(1175412139321702879)
XLA Ops:
  44.9 51.5 %while.26 = (s32[]{:T(128)}, bf16[2,1024,4,64]{1,3,2,0:T(8,128)(2,1)}, f32[2,4,1024]{2,1,0:T(4,128)S(1)}, bf16[2,1024,4,64]{1,3,2,0:T(8,128)(2,1)}, s32[2,1024]{...) while((s32[]{:T(128)}, ...), condition=%wide.region_3.4_spmd, body=%wide.region_0.3_spmd.sunk | while | flops 1112797184 | bytes 56768612 | solution.py:172
  53.1 8.8 fusion.154
  61.8 8.9 fusion.155
  78.7 8.8 fusion.154
  87.5 8.9 fusion.155
  106.4 153.3 %all-reduce.8.cloned.1.call-done = f32[2048,1024]{1,0:T(8,128)} async-done(((f32[2048,1024]{1,0:T(8,128)}), f32[2048,1024]{1,0:T(8,128)}) %all-reduce.8.cloned.1.call-update) | async-done | bytes 8388624 | tf_op jit(solution)/shard_map/psum | solution.py:175
  271.8 24.4 %multiply_convert_fusion.1 = (bf16[2048,1024]{1,0:T(8,128)(2,1)S(1)}, f32[2048,1024]{1,0:T(8,128)}, f32[2048,1024]{1,0:T(8,128)}) fusion(f32[1024]{0:T(1024)S(1)} %copy-done.69, bf16[1024,1024]{1,0:T(8,128)(2,1)S(1)} %copy-done.35, f32[2048,1024]{1,0:T(8,128)S(1)} %subtract_multiply_fusion.3, f32[1024]{0:T(1024)S(1)} %bitcast.355, f32[1024]{0:T(1024)S(1)} %bitcast.283), kind=kOutput, calls=%fused_computation.74 | convolution fusion | flops 4439670784 | bytes 31469568 | tf_op jit(solution)/shard_map/dot_general | solution.py:182
  304.9 153.1 %all-reduce.10.cloned.1.call-done = f32[2048,1024]{1,0:T(8,128)} async-done(((f32[2048,1024]{1,0:T(8,128)}), f32[2048,1024]{1,0:T(8,128)}) %all-reduce.10.cloned.1.call-update) | async-done | bytes 8388624 | tf_op jit(solution)/shard_map/psum | solution.py:188
  473.5 13.2 convert_reduce_fusion
  505.4 9.5 bitcast_add_fusion
  532.2 116.6 %all-reduce.12.cloned.1.call-done = f32[2048,1024]{1,0:T(8,128)} async-done(((f32[2048,1024]{1,0:T(8,128)}), f32[2048,1024]{1,0:T(8,128)}) %all-reduce.12.cloned.1.call-update) | async-done | bytes 8388624 | tf_op jit(solution)/shard_map/psum | solution.py:203
  648.8 11.4 multiply_reduce_fusion.5
  683.6 95.3 %while.27 = (s32[]{:T(128)}, bf16[2,1024,4,64]{1,3,2,0:T(8,128)(2,1)}, bf16[2,1024,4,64]{1,3,2,0:T(8,128)(2,1)}, bf16[2,1024,4,64]{1,3,2,0:T(8,128)(2,1)}, bf16[...) while((s32[]{:T(128)}, ...), condition=%wide.region_17.18_spmd, body=%wide.region_15.17_spmd.sunk | while | flops 2736517120 | bytes 219284944 | solution.py:211
  684.7 9.5 fusion.164
  694.2 8.8 fusion.167
  703.1 14.7 %multiply_reduce_fusion.152 = (f32[4,1024]{1,0:T(4,128)S(1)}, f32[4,1024,1024]{1,2,0:T(8,128)}) fusion(f32[4,1024,1024]{1,2,0:T(8,128)} %fusion.164, f32[4,1024]{1,0:T(4,128)S(1)} %dynamic-slice_bitcast_fusion.2, pred[1024,1024]{0,1:T(8,128)(4,1)} %copy-done.2, bf16[2,1024,4,64]{1,3,2,0:T(8,128)(2,1)} %get-tuple-element.794, s32[]{:T(128)S(6)} %copy.165, ...), kind=kOutput, calls=%fused_computation.22.clone.1 | convolution fusion | flops 553644032 | bytes 35685376 | tf_op jit(solution)/shard_map/while/body/eval_jaxpr/qhd,khd->hqk/dot_general | solution.py:97
  717.9 8.2 multiply_convert_fusion.5
  732.1 9.5 fusion.164
  741.7 8.9 fusion.167
  750.5 14.7 %multiply_reduce_fusion.152 = (f32[4,1024]{1,0:T(4,128)S(1)}, f32[4,1024,1024]{1,2,0:T(8,128)}) fusion(f32[4,1024,1024]{1,2,0:T(8,128)} %fusion.164, f32[4,1024]{1,0:T(4,128)S(1)} %dynamic-slice_bitcast_fusion.2, pred[1024,1024]{0,1:T(8,128)(4,1)} %copy-done.2, bf16[2,1024,4,64]{1,3,2,0:T(8,128)(2,1)} %get-tuple-element.794, s32[]{:T(128)S(6)} %copy.165, ...), kind=kOutput, calls=%fused_computation.22.clone.1 | convolution fusion | flops 553644032 | bytes 35685376 | tf_op jit(solution)/shard_map/while/body/eval_jaxpr/qhd,khd->hqk/dot_general | solution.py:97
  765.3 8.2 multiply_convert_fusion.5
  818.5 35.1 %all-reduce.2 = (bf16[256,8]{0,1:T(8,128)(2,1)S(1)}, bf16[1024,8]{0,1:T(8,128)(2,1)S(1)}, bf16[1024,8]{0,1:T(8,128)(2,1)S(1)}) all-reduce(bf16[256,8]{0,1:T(8,128)(2,1)S(1)} %convolution_convert_fusion.10, bf16[1024,8]{0,1:T(8,128)(2,1)S(1)} %copy-done.51, bf16[1024,8]{0,1:T(8,128)(2,1)S(1)} %copy-done.50), channel_id=1, replica_groups=mesh['dp'=8,'tensor'=4] {'dp'}, use_global_device_ids=true, to_apply=%region_60.61 | all-reduce | flops 18432 | bytes 73728 | tf_op jit(solution)/shard_map/psum | solution.py:276
  895.7 17.9 %subtract_divide_fusion.21 = (f32[256,1]{0,1:T(1,128)S(1)}, f32[256,1]{0,1:T(1,128)S(1)}, f32[256,1]{0,1:T(1,128)S(1)}, f32[256,1]{0,1:T(1,128)S(1)}, f32[256,1]...) fusion(f32[256,1]{0,1:T(1,128)S(1)} %get-tuple-element.612, f32[]{:T(128)S(6)} %add.369, ...), kind=kLoop, calls=%fused_computation.403 | loop fusion | flops 16128 | bytes 15500 | tf_op jit(solution)/shard_map/div | solution.py:69
  961.3 17.9 %subtract_divide_fusion = (f32[1024,1]{0,1:T(1,128)S(1)}, f32[1024,1]{0,1:T(1,128)S(1)}, f32[1024,1]{0,1:T(1,128)S(1)}, f32[1024,1]{0,1:T(1,128)S(1)}, f32[1024,...) fusion(f32[1024,1]{0,1:T(1,128)S(1)} %get-tuple-element.590, f32[]{:T(128)S(6)} %add.388, ...), kind=kLoop, calls=%fused_computation.160 | loop fusion | flops 64512 | bytes 61580 | tf_op jit(solution)/shard_map/div | solution.py:69
  1028.5 17.8 %subtract_divide_fusion.7 = (f32[1024,1]{0,1:T(1,128)S(1)}, f32[1024,1]{0,1:T(1,128)S(1)}, f32[1024,1]{0,1:T(1,128)S(1)}, f32[1024,1]{0,1:T(1,128)S(1)}, f32[102...) fusion(f32[1024,1]{0,1:T(1,128)S(1)} %get-tuple-element.598, f32[]{:T(128)S(6)} %add.378, ...), kind=kLoop, calls=%fused_computation.231 | loop fusion | flops 64512 | bytes 61580 | tf_op jit(solution)/shard_map/div | solution.py:69
  1051.5 43.7 %all-reduce = (f32[2,1024]{1,0:T(2,128)S(1)}, f32[4096]{0:T(1024)S(1)}, f32[6,1024]{1,0:T(8,128)S(1)}) all-reduce(f32[2,1024]{1,0:T(2,128)S(1)} %constant_dynamic-update-slice_fusion.3, f32[4096]{0:T(1024)S(1)} %copy-done.53, f32[6,1024]{1,0:T(8,128)S(1)} %stack.44), channel_id=1, replica_groups=mesh['dp'=8,'tensor'=4] {'dp','tensor'}, use_global_device_ids=true, to_apply=%region_59.60 | all-reduce | flops 12288 | bytes 98304 | tf_op jit(solution)/shard_map/psum | solution.py:257
  1096.5 7.5 bitcast_add_fusion.2
  1107.1 67.3 %all-reduce.14.cloned.1.call-done = (bf16[1024,8]{0,1:T(8,128)(2,1)}, bf16[8,1024]{1,0:T(8,128)(2,1)}, bf16[8,1024]{1,0:T(8,128)(2,1)}, bf16[8,1024]{1,0:T(8,128)(2,1)}) async-done(((bf16[1024,8]{0,1:T(8,128)(2,1)}, bf16[8,1024]{1,0:T(8,128)(2,1)}, bf16[8,1024]{1,0:T(8,128)(2,1)}, bf16[8,1024]{1,0:T(8,128)(2,1)}), (bf16[1024,8]{0,1:T(8,128)(2,1)}, bf16[8,1024]{1,0:T(8,128)(2,1)}, bf16[8,1024]{1,0:T(8,128)(2,1)}, ...) | async-done | bytes 65552 | tf_op jit(solution)/shard_map/psum | solution.py:272
  1220.9 18.0 %subtract_divide_fusion.14 = (f32[1024,1]{0,1:T(1,128)S(1)}, f32[1024,1]{0,1:T(1,128)S(1)}, f32[1024,1]{0,1:T(1,128)S(1)}, f32[1024,1]{0,1:T(1,128)S(1)}, f32[10...) fusion(f32[1024,1]{0,1:T(1,128)S(1)} %get-tuple-element.582, f32[]{:T(128)S(6)} %add.359, ...), kind=kLoop, calls=%fused_computation.301 | loop fusion | flops 64512 | bytes 61580 | tf_op jit(solution)/shard_map/div | solution.py:69
  1241.5 27.7 %all-gather = bf16[64,768]{1,0:T(8,128)(2,1)S(1)} all-gather(bf16[8,768]{1,0:T(8,128)(2,1)S(1)} %convolution_convert_fusion.9), channel_id=2, replica_groups=mesh['dp'=8,'tensor'=4] {'dp'}, dimensions={0}, use_global_device_ids=true | all-gather | bytes 110592 | tf_op jit(solution)/shard_map/all_gather | solution.py:286
  1297.3 12.1 multiply_subtract_fusion.1
  1309.4 12.1 multiply_subtract_fusion
  (387 shorter events, 417.8 us)
Async XLA Ops:
  7.2 509.6 %copy-start = (f32[8,1024]{1,0:T(8,128)S(1)}, f32[8,1024]{1,0:T(8,128)}, u32[]{:S(2)}) copy-start(f32[8,1024]{1,0:T(8,128)} %param.46) | copy-start | bytes 98308
  7.2 252.4 %all-reduce.8.cloned.1.call-start = ((), (), s32[]{:S(2)}) async-start(), calls=%async_computation.1 | async-start | bytes 16777216 | tf_op jit(solution)/shard_map/psum | solution.py:175
  106.3 351.8 %all-reduce.10.cloned.1.call-start = ((), (), s32[]{:S(2)}) async-start(), calls=%async_computation.2 | async-start | bytes 16777216 | tf_op jit(solution)/shard_map/psum | solution.py:188
  271.7 24.5 %copy-start.3 = (f32[2048,1024]{1,0:T(8,128)}, f32[2048,1024]{1,0:T(8,128)S(1)}, u32[]{:S(2)}) copy-start(f32[2048,1024]{1,0:T(8,128)S(1)} %subtract_multiply_fusion.3) | copy-start | bytes 25165828
  271.8 26.5 %copy-start.36 = (bf16[1024,1024]{1,0:T(8,128)(2,1)S(1)}, bf16[1024,1024]{1,0:T(8,128)(2,1)}, u32[]{:S(2)}) copy-start(bf16[1024,1024]{1,0:T(8,128)(2,1)} %param.36) | copy-start | bytes 6291460
  304.9 343.9 %all-reduce.12.cloned.1.call-start = ((), (), s32[]{:S(2)}) async-start(), calls=%async_computation.3 | async-start | bytes 16777216 | tf_op jit(solution)/shard_map/psum | solution.py:203
  495.6 678.8 %all-reduce.14.cloned.1.call-start = ((), (), s32[]{:S(2)}) async-start(), calls=%async_computation.5 | async-start | bytes 131072 | tf_op jit(solution)/shard_map/psum | solution.py:272
  500.8 20.2 %slice-start.4 = ((s8[8388608]{0:T(1024)(128)(4,1)}), s8[4194304]{0:T(1024)(128)(4,1)S(1)}, s32[]{:S(2)}) async-start(s8[8388608]{0:T(1024)(128)(4,1)} %bitcast.242), calls=%async_computation.10 | async-start | bytes 8388608
  505.4 15.6 %copy-start.75 = (bf16[2048,1024]{1,0:T(8,128)(2,1)S(1)}, bf16[2048,1024]{1,0:T(8,128)(2,1)}, u32[]{:S(2)}) copy-start(bf16[2048,1024]{1,0:T(8,128)(2,1)} %copy-done.74) | copy-start | bytes 12582916
  532.2 130.6 %copy-start.49 = (f32[2048]{0:T(1024)S(1)}, f32[2048]{0:T(1024)}, u32[]{:S(2)}) copy-start(f32[2048]{0:T(1024)} %copy-done.48) | copy-start | bytes 24580
  694.2 23.6 %slice-start = ((s8[16777216]{0:T(1024)(128)(4,1)}), s8[4194304]{0:T(1024)(128)(4,1)S(1)}, s32[]{:S(2)}) async-start(s8[16777216]{0:T(1024)(128)(4,1)} %bitcast.240), calls=%async_computation.6 | async-start | bytes 8388608 | tf_op jit(solution)/shard_map/while
  694.2 23.6 %slice-start.1 = ((s8[16777216]{0:T(1024)(128)(4,1)}), s8[4194304]{0:T(1024)(128)(4,1)S(1)}, s32[]{:S(2)}) async-start(s8[16777216]{0:T(1024)(128)(4,1)} %bitcast.240), calls=%async_computation.7 | async-start | bytes 8388608 | tf_op jit(solution)/shard_map/while
  741.7 23.6 %slice-start = ((s8[16777216]{0:T(1024)(128)(4,1)}), s8[4194304]{0:T(1024)(128)(4,1)S(1)}, s32[]{:S(2)}) async-start(s8[16777216]{0:T(1024)(128)(4,1)} %bitcast.240), calls=%async_computation.6 | async-start | bytes 8388608 | tf_op jit(solution)/shard_map/while
  741.7 23.6 %slice-start.1 = ((s8[16777216]{0:T(1024)(128)(4,1)}), s8[4194304]{0:T(1024)(128)(4,1)S(1)}, s32[]{:S(2)}) async-start(s8[16777216]{0:T(1024)(128)(4,1)} %bitcast.240), calls=%async_computation.7 | async-start | bytes 8388608 | tf_op jit(solution)/shard_map/while
  813.6 237.7 %copy-start.58 = (f32[1024]{0:T(1024)S(1)}, f32[1024]{0:T(1024)}, u32[]{:S(2)}) copy-start(f32[1024]{0:T(1024)} %get-tuple-element.622) | copy-start | bytes 12292
  813.6 237.7 %copy-start.59 = (f32[1024]{0:T(1024)S(1)}, f32[1024]{0:T(1024)}, u32[]{:S(2)}) copy-start(f32[1024]{0:T(1024)} %get-tuple-element.623) | copy-start | bytes 12292
  813.7 237.7 %copy-start.63 = (f32[1024]{0:T(1024)S(1)}, f32[1024]{0:T(1024)}, u32[]{:S(2)}) copy-start(f32[1024]{0:T(1024)} %get-tuple-element.278) | copy-start | bytes 12292
  813.7 237.7 %copy-start.64 = (f32[1024]{0:T(1024)S(1)}, f32[1024]{0:T(1024)}, u32[]{:S(2)}) copy-start(f32[1024]{0:T(1024)} %get-tuple-element.279) | copy-start | bytes 12292
  813.7 237.7 %copy-start.65 = (f32[1024]{0:T(1024)S(1)}, f32[1024]{0:T(1024)}, u32[]{:S(2)}) copy-start(f32[1024]{0:T(1024)} %get-tuple-element.274) | copy-start | bytes 12292
  813.7 237.7 %copy-start.66 = (f32[1024]{0:T(1024)S(1)}, f32[1024]{0:T(1024)}, u32[]{:S(2)}) copy-start(f32[1024]{0:T(1024)} %get-tuple-element.275) | copy-start | bytes 12292
  813.7 237.8 %copy-start.53 = (f32[4096]{0:T(1024)S(1)}, f32[4096]{0:T(1024)}, u32[]{:S(2)}) copy-start(f32[4096]{0:T(1024)} %copy-done.52) | copy-start | bytes 49156
  817.5 278.9 %copy-start.18 = (f32[256,1024]{1,0:T(8,128)}, f32[256,1024]{1,0:T(8,128)S(1)}, u32[]{:S(2)}) copy-start(f32[256,1024]{1,0:T(8,128)S(1)} %convolution_add_fusion) | copy-start | bytes 3145732
  817.5 277.6 %copy-start.70 = (f32[1024]{0:T(1024)S(1)}, f32[1024]{0:T(1024)}, u32[]{:S(2)}) copy-start(f32[1024]{0:T(1024)} %param.35) | copy-start | bytes 12292
  817.6 277.6 %copy-start.71 = (f32[1024]{0:T(1024)S(1)}, f32[1024]{0:T(1024)}, u32[]{:S(2)}) copy-start(f32[1024]{0:T(1024)} %param.51) | copy-start | bytes 12292
  817.6 278.2 %copy-start.47 = (f32[6,1024]{1,0:T(8,128)S(1)}, f32[6,1024]{1,0:T(8,128)}, u32[]{:S(2)}) copy-start(f32[6,1024]{1,0:T(8,128)} %param.37) | copy-start | bytes 73732
  817.6 278.2 %copy-start.56 = (f32[6,1024]{1,0:T(8,128)S(1)}, f32[6,1024]{1,0:T(8,128)}, u32[]{:S(2)}) copy-start(f32[6,1024]{1,0:T(8,128)} %param.53) | copy-start | bytes 73732
  1106.4 215.1 %reduce-scatter.2.cloned.1.call-start = ((), (), s32[]{:S(2)}) async-start(), calls=%async_computation.4 | async-start | bytes 5242880 | tf_op jit(solution)/shard_map/reduce_scatter | solution.py:230
  1280.1 17.2 %copy-start.17 = (f32[1024,3,256]{2,0,1:T(8,128)}, f32[1024,3,256]{2,0,1:T(8,128)S(1)}, u32[]{:S(2)}) copy-start(f32[1024,3,256]{2,0,1:T(8,128)S(1)} %copy.125) | copy-start | bytes 9437188
  1280.8 16.5 %copy-start.45 = (f32[8,1024]{1,0:T(8,128)}, f32[8,1024]{1,0:T(8,128)S(1)}, u32[]{:S(2)}) copy-start(f32[8,1024]{1,0:T(8,128)S(1)} %convert_multiply_fusion.6) | copy-start | bytes 98308
  1280.8 16.5 %copy-start.43 = (f32[8,1024]{1,0:T(8,128)}, f32[8,1024]{1,0:T(8,128)S(1)}, u32[]{:S(2)}) copy-start(f32[8,1024]{1,0:T(8,128)S(1)} %convert_multiply_fusion.4) | copy-start | bytes 98308
  1280.9 16.4 %copy-start.44 = (f32[8,1024]{1,0:T(8,128)}, f32[8,1024]{1,0:T(8,128)S(1)}, u32[]{:S(2)}) copy-start(f32[8,1024]{1,0:T(8,128)S(1)} %convert_multiply_fusion.2) | copy-start | bytes 98308
  1309.4 15.7 %copy-start.1 = (f32[8,1024]{1,0:T(8,128)S(1)}, f32[8,1024]{1,0:T(8,128)}, u32[]{:S(2)}) copy-start(f32[8,1024]{1,0:T(8,128)} %param.46) | copy-start | bytes 98308
  (67 other events, 491.7 us)
Sparse Core Ops, SparseCore 0:
  106.4 153.2 all-reduce.7
  305.0 153.0 all-reduce.9
  495.8 153.0 all-reduce.11
  1106.5 67.8 all-reduce.13
  1176.8 43.4 reduce-scatter.1
